TPU v7x, 32 devices: a whole 2x2x4 slice. The times are simulated.
32 devices in a mesh: dp: 4 (over x, core), ctx: 2 (over y), tensor: 4 (over z).
Axes of the slice: x: 2, y: 2, z: 4, core: 2. Of those that a mesh axis runs over, the one named last changes fastest.
Arguments:
- inputs: bfloat16 [2048, 2048], P(('dp', 'ctx'), 'tensor'), may hold values from -6 to 6
- cotangent: bfloat16 [2048, 2048], P(('dp', 'ctx')), may hold values from -6 to 6
- segments: int32 [4, 512], P('dp'), may hold values from 0 to 15, as said below
- positions: int32 [4, 512], P('dp', 'ctx'), may hold values from 0 to 511, as said below
- attention_gain: bfloat16 [2048], replicated, may hold values from 0.5 to 1.5
- query_weight: bfloat16 [2048, 2048], P(None, 'tensor'), may hold values from -0.125 to 0.125
- key_weight: bfloat16 [2048, 1024], P(None, 'tensor'), may hold values from -0.125 to 0.125
- value_weight: bfloat16 [2048, 1024], P(None, 'tensor'), may hold values from -0.125 to 0.125
- query_gain: bfloat16 [128], replicated, may hold values from 0.5 to 1.5
- key_gain: bfloat16 [128], replicated, may hold values from 0.5 to 1.5
- output_weight: bfloat16 [2048, 2048], P('tensor'), may hold values from -0.75 to 0.75
- feed_gain: bfloat16 [2048], replicated, may hold values from 0.3 to 5, as said below
- gate_weight: bfloat16 [2048, 6144], P(None, 'tensor'), may hold values from -0.125 to 0.125
- up_weight: bfloat16 [2048, 6144], P(None, 'tensor'), may hold values from -0.125 to 0.125
- down_weight: bfloat16 [6144, 2048], P('tensor'), may hold values from -0.078125 to 0.078125
Outputs:
- outputs: bfloat16 [2048, 2048], P(('dp', 'ctx'), 'tensor')
- grad_inputs: float32 [2048, 2048], P(('dp', 'ctx'), 'tensor')
- grad_attention_gain: float32 [2048], P('tensor')
- grad_query_weight: float32 [2048, 2048], P(None, 'tensor')
- grad_key_weight: float32 [2048, 1024], P(None, 'tensor')
- grad_value_weight: float32 [2048, 1024], P(None, 'tensor')
- grad_query_gain: float32 [128], replicated
- grad_key_gain: float32 [128], replicated
- grad_output_weight: float32 [2048, 2048], P('tensor')
- grad_feed_gain: float32 [2048], P('tensor')
- grad_gate_weight: float32 [2048, 6144], P(None, 'tensor')
- grad_up_weight: float32 [2048, 6144], P(None, 'tensor')
- grad_down_weight: float32 [6144, 2048], P('tensor')
Inputs may be any that keep to these rules, and one draw needn't show every extreme that they name: `segments`: in each sequence the document numbers start at 0, never fall, and each document is one run of equal numbers; a sequence holds at most 16 documents. `positions`: a token's position counts from 0 at the first token of its document. `feed_gain`: positive gains.
All inputs are finite; a program needn't handle non-finite values.
Results may differ from a plain program's by a relative error of at most 0.024.
Values may be sent and summed in bfloat16 or wider, within the bound.
No kernel may reach another device: no remote copies, remote signals or barrier semaphores. Data moves between devices by JAX's collectives and lax.ppermute only.
A program may use at most 256 MiB of HBM per device.

v0:
```python
import jax
import jax.numpy as jnp
from jax import lax
from jax.sharding import PartitionSpec as P

HD = 128
EPS = 1e-06
THETA = 1000000.0
NEG = -1e30


def rope_tables(position_row):
    half = HD // 2
    freqs = jnp.exp(-(2.0 * jnp.arange(half, dtype=jnp.float32) / HD) * jnp.log(jnp.float32(THETA)))
    angles = position_row.astype(jnp.float32)[:, None] * freqs[None, :]
    return (jnp.cos(angles)[:, None, :], jnp.sin(angles)[:, None, :])


def rotate(value, cosine, sine):
    half = value.shape[-1] // 2
    first = value[..., :half]
    second = value[..., half:]
    return jnp.concatenate(
        [first * cosine - second * sine, second * cosine + first * sine], axis=-1
    )


def head_prepare(raw, gain, cosine, sine):
    count = raw.shape[0]
    heads = raw.reshape(count, -1, HD)
    normed = heads * lax.rsqrt(jnp.mean(heads * heads, axis=-1, keepdims=True) + EPS) * gain
    return rotate(normed, cosine, sine).reshape(count, -1)


def matmul(left, right):
    return jnp.dot(left, right, preferred_element_type=jnp.float32)


def per_device(
    inputs,
    cotangent,
    segments,
    positions,
    attention_gain,
    query_weight,
    key_weight,
    value_weight,
    query_gain,
    key_gain,
    output_weight,
    feed_gain,
    gate_weight,
    up_weight,
    down_weight,
):
    count = inputs.shape[0]
    shard = inputs.shape[1]
    width = cotangent.shape[1]
    column = lax.axis_index("tensor") * shard
    place = lax.axis_index("ctx")
    kv_local = key_weight.shape[1] // HD
    group = query_weight.shape[1] // key_weight.shape[1]
    factor = HD ** (-0.5)
    block = min(512, count)
    blocks = count // block
    gain_one = attention_gain.astype(jnp.float32)
    gain_two = feed_gain.astype(jnp.float32)
    gain_one_part = lax.dynamic_slice_in_dim(gain_one, column, shard)
    gain_two_part = lax.dynamic_slice_in_dim(gain_two, column, shard)
    cosine, sine = rope_tables(positions[0])
    gathered = lax.all_gather(inputs, "tensor", axis=1, tiled=True).astype(jnp.float32)
    inverse_one = lax.rsqrt(jnp.mean(gathered * gathered, axis=-1, keepdims=True) + EPS)
    unit_one = gathered * inverse_one
    normed_one = (unit_one * gain_one).astype(jnp.bfloat16)
    query_raw = matmul(normed_one, query_weight)
    key_raw = matmul(normed_one, key_weight)
    value_rows = matmul(normed_one, value_weight).astype(jnp.bfloat16)
    query_float, query_pull = jax.vjp(
        lambda raw, gain: head_prepare(raw, gain, cosine, sine),
        query_raw,
        query_gain.astype(jnp.float32),
    )
    key_float, key_pull = jax.vjp(
        lambda raw, gain: head_prepare(raw, gain, cosine, sine),
        key_raw,
        key_gain.astype(jnp.float32),
    )
    query_rows = query_float.astype(jnp.bfloat16)
    key_rows = key_float.astype(jnp.bfloat16)
    segment_row = segments[0]
    all_keys, all_values = (
        lax.all_gather(key_rows, "ctx", axis=0, tiled=True),
        lax.all_gather(value_rows, "ctx", axis=0, tiled=True),
    )
    total_keys = all_keys.shape[0]
    key_index = jnp.arange(total_keys, dtype=jnp.int32)
    row_offset = place * count
    key_heads = all_keys.reshape(total_keys, kv_local, HD)
    value_heads = all_values.reshape(total_keys, kv_local, HD)
    query_blocks = query_rows.reshape(blocks, block, kv_local, group, HD)

    def allowed_mask(index):
        start = index * block
        row_index = row_offset + start + jnp.arange(block, dtype=jnp.int32)
        row_segment = lax.dynamic_slice_in_dim(segment_row, row_offset + start, block)
        return (row_segment[:, None] == segment_row[None, :]) & (
            key_index[None, :] <= row_index[:, None]
        )

    def block_scores(rows, index):
        scores = (
            jnp.einsum("qhgd,khd->hgqk", rows, key_heads, preferred_element_type=jnp.float32)
            * factor
        )
        return jnp.where(allowed_mask(index)[None, None], scores, NEG)

    def forward_block(index):
        rows = query_blocks[index]
        scores = block_scores(rows, index)
        top = jnp.max(scores, axis=-1, keepdims=True)
        raised = jnp.exp(scores - top)
        total = jnp.sum(raised, axis=-1, keepdims=True)
        weights = (raised / total).astype(jnp.bfloat16)
        mixed = jnp.einsum(
            "hgqk,khd->qhgd", weights, value_heads, preferred_element_type=jnp.float32
        )
        return (mixed.astype(jnp.bfloat16), top + jnp.log(total))

    mixed_blocks, log_totals = lax.map(forward_block, jnp.arange(blocks, dtype=jnp.int32))
    mixed_rows = mixed_blocks.reshape(count, -1)
    attention_terms = matmul(mixed_rows, output_weight)
    branch = lax.psum_scatter(attention_terms, "tensor", scatter_dimension=1, tiled=True)
    resid_part = (inputs.astype(jnp.float32) + branch).astype(jnp.bfloat16)
    resid_rows = lax.all_gather(resid_part, "tensor", axis=1, tiled=True).astype(jnp.float32)
    inverse_two = lax.rsqrt(jnp.mean(resid_rows * resid_rows, axis=-1, keepdims=True) + EPS)
    unit_two = resid_rows * inverse_two
    normed_two = (unit_two * gain_two).astype(jnp.bfloat16)
    gate = matmul(normed_two, gate_weight)
    up_rows = matmul(normed_two, up_weight)
    sigmoid = jax.nn.sigmoid(gate)
    silu = gate * sigmoid
    hidden = (silu * up_rows).astype(jnp.bfloat16)
    feed = lax.psum_scatter(
        matmul(hidden, down_weight).astype(jnp.bfloat16), "tensor", scatter_dimension=1, tiled=True
    ).astype(jnp.float32)
    outputs = (resid_part.astype(jnp.float32) + feed).astype(jnp.bfloat16)
    grad_down = matmul(hidden.T, cotangent)
    grad_hidden = matmul(cotangent, down_weight.T)
    grad_gate = (grad_hidden * up_rows * sigmoid * (1.0 + gate * (1.0 - sigmoid))).astype(
        jnp.bfloat16
    )
    grad_up = (grad_hidden * silu).astype(jnp.bfloat16)
    grad_gate_w = matmul(normed_two.T, grad_gate)
    grad_up_w = matmul(normed_two.T, grad_up)
    grad_normed_two = matmul(grad_gate, gate_weight.T) + matmul(grad_up, up_weight.T)
    unit_two_part = lax.dynamic_slice_in_dim(unit_two, column, shard, 1)
    grad_out_part = lax.dynamic_slice_in_dim(cotangent, column, shard, 1).astype(jnp.float32)
    grad_two_part = lax.psum_scatter(grad_normed_two, "tensor", scatter_dimension=1, tiled=True)
    row_term_two = jnp.sum(gain_two_part * grad_two_part * unit_two_part, axis=-1)
    row_total_two = lax.psum(row_term_two, "tensor")
    grad_feed_gain = jnp.sum(grad_two_part * unit_two_part, axis=0)
    grad_resid = (
        grad_out_part
        + inverse_two * (gain_two_part * grad_two_part)
        - unit_two_part * (inverse_two / width) * row_total_two[:, None]
    )
    grad_resid_rows = lax.all_gather(grad_resid.astype(jnp.bfloat16), "tensor", axis=1, tiled=True)
    grad_output_w = matmul(mixed_rows.T, grad_resid_rows)
    grad_mixed = matmul(grad_resid_rows, output_weight.T).astype(jnp.bfloat16)
    grad_mixed_blocks = grad_mixed.reshape(blocks, block, kv_local, group, HD)

    def backward_block(carry, index):
        key_total, value_total = carry
        rows = query_blocks[index]
        grad_rows = grad_mixed_blocks[index]
        scores = block_scores(rows, index)
        probs = jnp.exp(scores - log_totals[index])
        grad_probs = jnp.einsum(
            "qhgd,khd->hgqk", grad_rows, value_heads, preferred_element_type=jnp.float32
        )
        delta = jnp.sum(probs * grad_probs, axis=-1, keepdims=True)
        grad_scores = (probs * (grad_probs - delta)).astype(jnp.bfloat16)
        grad_query = (
            jnp.einsum("hgqk,khd->qhgd", grad_scores, key_heads, preferred_element_type=jnp.float32)
            * factor
        )
        key_total = (
            key_total
            + jnp.einsum("hgqk,qhgd->khd", grad_scores, rows, preferred_element_type=jnp.float32)
            * factor
        )
        value_total = value_total + jnp.einsum(
            "hgqk,qhgd->khd",
            probs.astype(jnp.bfloat16),
            grad_rows,
            preferred_element_type=jnp.float32,
        )
        return ((key_total, value_total), grad_query)

    empty = jnp.zeros((total_keys, kv_local, HD), jnp.float32)
    (key_total, value_total), grad_query_blocks = lax.scan(
        backward_block, (empty, empty), jnp.arange(blocks, dtype=jnp.int32)
    )
    grad_query_rows = grad_query_blocks.reshape(count, -1)
    key_total = key_total.reshape(total_keys, -1)
    value_total = value_total.reshape(total_keys, -1)
    grad_key_rot, grad_value = (
        lax.psum_scatter(
            key_total.astype(jnp.bfloat16), "ctx", scatter_dimension=0, tiled=True
        ).astype(jnp.float32),
        lax.psum_scatter(
            value_total.astype(jnp.bfloat16), "ctx", scatter_dimension=0, tiled=True
        ).astype(jnp.float32),
    )
    grad_query_raw, grad_query_gain = query_pull(grad_query_rows)
    grad_key_raw, grad_key_gain = key_pull(grad_key_rot)
    grad_query_low = grad_query_raw.astype(jnp.bfloat16)
    grad_key_low = grad_key_raw.astype(jnp.bfloat16)
    grad_value_low = grad_value.astype(jnp.bfloat16)
    grad_query_w = matmul(normed_one.T, grad_query_low)
    grad_key_w = matmul(normed_one.T, grad_key_low)
    grad_value_w = matmul(normed_one.T, grad_value_low)
    grad_normed_one = (
        matmul(grad_query_low, query_weight.T)
        + matmul(grad_key_low, key_weight.T)
        + matmul(grad_value_low, value_weight.T)
    )
    grad_one_part = lax.psum_scatter(
        grad_normed_one.astype(jnp.bfloat16), "tensor", scatter_dimension=1, tiled=True
    ).astype(jnp.float32)
    unit_one_part = lax.dynamic_slice_in_dim(unit_one, column, shard, 1)
    row_term_one = jnp.sum(gain_one_part * grad_one_part * unit_one_part, axis=-1)
    row_total_one, query_gain_total, key_gain_total = lax.psum(
        (row_term_one, grad_query_gain, grad_key_gain), "tensor"
    )
    grad_inputs = (
        grad_resid
        + inverse_one * (gain_one_part * grad_one_part)
        - unit_one_part * (inverse_one / width) * row_total_one[:, None]
    )
    grad_attention_gain = jnp.sum(grad_one_part * unit_one_part, axis=0)
    summed = (
        lax.psum(grad_attention_gain.astype(jnp.bfloat16), ("dp", "ctx")).astype(jnp.float32),
        lax.psum(grad_query_w.astype(jnp.bfloat16), ("dp", "ctx")).astype(jnp.float32),
        lax.psum(grad_key_w.astype(jnp.bfloat16), ("dp", "ctx")).astype(jnp.float32),
        lax.psum(grad_value_w.astype(jnp.bfloat16), ("dp", "ctx")).astype(jnp.float32),
        lax.psum(query_gain_total.astype(jnp.bfloat16), ("dp", "ctx")).astype(jnp.float32),
        lax.psum(key_gain_total.astype(jnp.bfloat16), ("dp", "ctx")).astype(jnp.float32),
        lax.psum(grad_output_w.astype(jnp.bfloat16), ("dp", "ctx")).astype(jnp.float32),
        lax.psum(grad_feed_gain.astype(jnp.bfloat16), ("dp", "ctx")).astype(jnp.float32),
        lax.psum(grad_gate_w.astype(jnp.bfloat16), ("dp", "ctx")).astype(jnp.float32),
        lax.psum(grad_up_w.astype(jnp.bfloat16), ("dp", "ctx")).astype(jnp.float32),
        lax.psum(grad_down.astype(jnp.bfloat16), ("dp", "ctx")).astype(jnp.float32),
    )
    return (outputs, grad_inputs) + tuple(summed)


def solution(mesh):
    in_specs = (
        P(("dp", "ctx"), "tensor"),
        P(("dp", "ctx"), None),
        P("dp", None),
        P("dp", "ctx"),
        P(),
        P(None, "tensor"),
        P(None, "tensor"),
        P(None, "tensor"),
        P(),
        P(),
        P("tensor", None),
        P(),
        P(None, "tensor"),
        P(None, "tensor"),
        P("tensor", None),
    )
    out_specs = (
        P(("dp", "ctx"), "tensor"),
        P(("dp", "ctx"), "tensor"),
        P("tensor"),
        P(None, "tensor"),
        P(None, "tensor"),
        P(None, "tensor"),
        P(),
        P(),
        P("tensor", None),
        P("tensor"),
        P(None, "tensor"),
        P(None, "tensor"),
        P("tensor", None),
    )
    return jax.shard_map(
        per_device, mesh=mesh, in_specs=in_specs, out_specs=out_specs, check_vma=False
    )
```

profile of v0, /device:TPU:0, one launch (start us, length us, event | category | flops | bytes accessed | tf_op | source)
XLA Modules:
  0.0 697.9 jit_solution(3110859281240040887)
XLA Ops:
  15.3 24.9 %all-gather.4.cloned.1.call-done = bf16[256,2048]{1,0:T(8,128)(2,1)} async-done(((bf16[256,512]{1,0:T(8,128)(2,1)}), bf16[256,2048]{1,0:T(8,128)(2,1)}) %all-gather.4.cloned.1.call-update) | async-done | bytes 1048592 | tf_op jit(solution)/shard_map/all_gather | solution.py:71
  44.4 5.8 all_gather.16
  54.4 5.8 all_gather.17
  70.3 43.7 %reduce-scatter.7.cloned.1.call-done = f32[256,512]{1,0:T(8,128)} async-done(((f32[256,2048]{1,0:T(8,128)}), f32[256,512]{1,0:T(8,128)}) %reduce-scatter.7.cloned.1.call-update) | async-done | bytes 524304 | tf_op jit(solution)/shard_map/reduce_scatter | solution.py:132
  116.3 27.0 %all-gather.6.cloned.1.call-done = bf16[256,2048]{1,0:T(8,128)(2,1)} async-done(((bf16[256,512]{1,0:T(8,128)(2,1)}), bf16[256,2048]{1,0:T(8,128)(2,1)}) %all-gather.6.cloned.1.call-update) | async-done | bytes 1048592 | tf_op jit(solution)/shard_map/all_gather | solution.py:134
  145.6 5.8 fusion.33
  153.4 3.3 multiply_convert_fusion.2
  158.6 3.2 convolution_add_fusion.1
  164.1 41.2 %reduce-scatter.11.cloned.1.call-done = f32[256,512]{1,0:T(8,128)} async-done(((f32[256,2048]{1,0:T(8,128)}), f32[256,512]{1,0:T(8,128)}) %reduce-scatter.11.cloned.1.call-update) | async-done | bytes 524304 | tf_op jit(solution)/shard_map/reduce_scatter | solution.py:158
  207.2 10.5 %psum.105 = f32[256]{0:T(256)} all-reduce(f32[256]{0:T(256)} %get-tuple-element.70), channel_id=1, replica_groups=mesh['dp'=4,'ctx'=2,'tensor'=4] {'tensor'}, use_global_device_ids=true, to_apply=%region_10.11 | all-reduce | flops 256 | bytes 2048 | tf_op jit(solution)/shard_map/psum | solution.py:160
  220.9 25.7 %all-gather.8.cloned.1.call-done = bf16[256,2048]{1,0:T(8,128)(2,1)} async-done(((bf16[256,512]{1,0:T(8,128)(2,1)}), bf16[256,2048]{1,0:T(8,128)(2,1)}) %all-gather.8.cloned.1.call-update) | async-done | bytes 1048592 | tf_op jit(solution)/shard_map/all_gather | solution.py:167
  258.4 10.1 %reduce-scatter.9.cloned.1.call-start = ((), (), s32[]{:S(2)}) async-start(), calls=%async_computation.9 | async-start | bytes 1310720 | tf_op jit(solution)/shard_map/reduce_scatter | solution.py:143
  268.5 5.9 convolution_convert_fusion.7
  288.9 6.1 convolution_convert_fusion
  294.9 4.7 convolution_convert_fusion.1
  299.6 4.7 convolution_convert_fusion.2
  315.0 25.9 %reduce-scatter.17.cloned.1.call-done = bf16[256,512]{1,0:T(8,128)(2,1)} async-done(((bf16[256,2048]{1,0:T(8,128)(2,1)}), bf16[256,512]{1,0:T(8,128)(2,1)}) %reduce-scatter.17.cloned.1.call-update) | async-done | bytes 262160 | tf_op jit(solution)/shard_map/reduce_scatter | solution.py:228
  342.1 9.7 %all-reduce.4 = (f32[256]{0:T(256)S(1)}, bf16[128]{0:T(256)(128)(2,1)S(1)}, bf16[128]{0:T(256)(128)(2,1)S(1)}) all-reduce(f32[256]{0:T(256)S(1)} %get-tuple-element.72, f32[128]{0:T(128)S(1)} %copy-done.63, f32[128]{0:T(128)S(1)} %copy-done.64), channel_id=1, replica_groups=mesh['dp'=4,'ctx'=2,'tensor'=4] {'tensor'}, use_global_device_ids=true, to_apply=%region_18.19 | all-reduce | flops 512 | bytes 3584 | tf_op jit(solution)/shard_map/psum | solution.py:233
  351.8 14.3 %all-reduce.5 = (bf16[512]{0:T(512)(128)(2,1)S(1)}, bf16[128]{0:T(256)(128)(2,1)S(1)}, bf16[128]{0:T(256)(128)(2,1)S(1)}, bf16[512]{0:T(512)(128)(2,1)S(1)}) all-reduce(bf16[512]{0:T(512)(128)(2,1)S(1)} %get-tuple-element.71, bf16[128]{0:T(256)(128)(2,1)S(1)} %get-tuple-element.78, ...), channel_id=1, replica_groups=mesh['dp'=4,'ctx'=2,'tensor'=4] {'dp','ctx'}, use_global_device_ids=true, to_apply=%region_20.21 | all-reduce | flops 1280 | bytes 5120 | tf_op jit(solution)/shard_map/psum | solution.py:243
  370.4 287.2 %all-reduce.9.cloned.1.call-done = (bf16[2048,512]{1,0:T(8,128)(2,1)}, bf16[2048,256]{1,0:T(8,128)(2,1)}, bf16[2048,256]{1,0:T(8,128)(2,1)}, bf16[512,2048]{1,0:...) async-done(((bf16[2048,512]{1,0:T(8,128)(2,1)}, bf16[2048,256]{1,0:T(8,128)(2,1)}, bf16[2048,256]{1,0:T(8,128)(2,1)}, ...) | async-done | bytes 25165840 | tf_op jit(solution)/shard_map/psum | solution.py:244
  657.6 4.3 convert_element_type.251
  668.4 9.5 %convert_element_type.265 = f32[2048,1536]{1,0:T(8,128)} convert(bf16[2048,1536]{1,0:T(8,128)(2,1)} %get-tuple-element.101) | non-fusion elementwise | flops 3145728 | bytes 18874368 | tf_op jit(solution)/shard_map/convert_element_type | solution.py:251
  677.9 6.6 convert_element_type.267
  684.5 6.3 convert_element_type.269
  (262 shorter events, 90.6 us)
Async XLA Ops:
  7.2 61.0 %copy-start = (bf16[512,2048]{1,0:T(8,128)(2,1)S(1)}, bf16[512,2048]{1,0:T(8,128)(2,1)}, u32[]{:S(2)}) copy-start(bf16[512,2048]{1,0:T(8,128)(2,1)} %param.25) | copy-start | bytes 6291460
  7.2 33.1 %all-gather.4.cloned.1.call-start = ((), (), s32[]{:S(2)}) async-start(), calls=%async_computation.6 | async-start | bytes 1310720 | tf_op jit(solution)/shard_map/all_gather | solution.py:71
  7.9 106.1 %reduce-scatter.7.cloned.1.call-start = ((), (), s32[]{:S(2)}) async-start(), calls=%async_computation.7 | async-start | bytes 2621440 | tf_op jit(solution)/shard_map/reduce_scatter | solution.py:132
  8.6 55.5 %copy-start.58 = (f32[128]{0:T(128)}, f32[128]{0:T(128)S(1)}, u32[]{:S(2)}) copy-start(f32[128]{0:T(128)S(1)} %convert_element_type.215) | copy-start | bytes 1540
  11.2 49.0 %copy-start.56 = (f32[2048]{0:T(1024)}, f32[2048]{0:T(1024)S(1)}, u32[]{:S(2)}) copy-start(f32[2048]{0:T(1024)S(1)} %convert_element_type.208) | copy-start | bytes 24580
  11.7 28.5 %copy-start.16 = (f32[256,64]{1,0:T(8,128)}, f32[256,64]{1,0:T(8,128)S(1)}, u32[]{:S(2)}) copy-start(f32[256,64]{1,0:T(8,128)S(1)} %get-tuple-element.120) | copy-start | bytes 196612
  42.3 17.8 %copy-start.50 = (f32[256]{0:T(256)}, f32[256]{0:T(256)S(1)}, u32[]{:S(2)}) copy-start(f32[256]{0:T(256)S(1)} %get-tuple-element.122) | copy-start | bytes 3076
  70.2 43.8 %copy-start.30 = (bf16[256,512]{1,0:T(8,128)(2,1)S(1)}, bf16[256,512]{1,0:T(8,128)(2,1)}, u32[]{:S(2)}) copy-start(bf16[256,512]{1,0:T(8,128)(2,1)} %param.15) | copy-start | bytes 786436
  70.2 46.1 %copy-start.52 = (bf16[2048]{0:T(1024)(128)(2,1)S(1)}, bf16[2048]{0:T(1024)(128)(2,1)}, u32[]{:S(2)}) copy-start(bf16[2048]{0:T(1024)(128)(2,1)} %param.26) | copy-start | bytes 12292
  70.3 73.0 %all-gather.6.cloned.1.call-start = ((), (), s32[]{:S(2)}) async-start(), calls=%async_computation.8 | async-start | bytes 1310720 | tf_op jit(solution)/shard_map/all_gather | solution.py:134
  115.9 89.4 %reduce-scatter.11.cloned.1.call-start = ((), (), s32[]{:S(2)}) async-start(), calls=%async_computation.10 | async-start | bytes 2621440 | tf_op jit(solution)/shard_map/reduce_scatter | solution.py:158
  143.3 10.0 %slice-start.8 = ((s8[6291456]{0:T(1024)(128)(4,1)}), s8[4194304]{0:T(1024)(128)(4,1)S(1)}, s32[]{:S(2)}) async-start(s8[6291456]{0:T(1024)(128)(4,1)} %bitcast.136), calls=%async_computation.24 | async-start | bytes 8388608
  161.8 84.8 %all-gather.8.cloned.1.call-start = ((), (), s32[]{:S(2)}) async-start(), calls=%async_computation.11 | async-start | bytes 1310720 | tf_op jit(solution)/shard_map/all_gather | solution.py:167
  220.1 62.4 %reduce-scatter.13.cloned.1.call-start = ((), (), s32[]{:S(2)}) async-start(), calls=%async_computation.12 | async-start | bytes 393216 | tf_op jit(solution)/shard_map/reduce_scatter | solution.py:208
  256.2 28.8 %reduce-scatter.15.cloned.1.call-start = ((), (), s32[]{:S(2)}) async-start(), calls=%async_computation.13 | async-start | bytes 393216 | tf_op jit(solution)/shard_map/reduce_scatter | solution.py:211
  258.4 54.3 %reduce-scatter.9.cloned.1.call-start = ((), (), s32[]{:S(2)}) async-start(), calls=%async_computation.9 | async-start | bytes 1310720 | tf_op jit(solution)/shard_map/reduce_scatter | solution.py:143
  274.4 66.5 %reduce-scatter.17.cloned.1.call-start = ((), (), s32[]{:S(2)}) async-start(), calls=%async_computation.14 | async-start | bytes 1310720 | tf_op jit(solution)/shard_map/reduce_scatter | solution.py:228
  288.8 368.8 %all-reduce.9.cloned.1.call-start = ((), (), s32[]{:S(2)}) async-start(), calls=%async_computation.15 | async-start | bytes 50331648 | tf_op jit(solution)/shard_map/psum | solution.py:244
  312.4 29.6 %copy-start.63 = (f32[128]{0:T(128)S(1)}, f32[128]{0:T(128)}, u32[]{:S(2)}) copy-start(f32[128]{0:T(128)} %get-tuple-element.73) | copy-start | bytes 1540
  312.4 29.6 %copy-start.64 = (f32[128]{0:T(128)S(1)}, f32[128]{0:T(128)}, u32[]{:S(2)}) copy-start(f32[128]{0:T(128)} %get-tuple-element.75) | copy-start | bytes 1540
  312.4 39.4 %copy-start.62 = (bf16[512]{0:T(512)(128)(2,1)S(1)}, bf16[512]{0:T(512)(128)(2,1)}, u32[]{:S(2)}) copy-start(bf16[512]{0:T(512)(128)(2,1)} %get-tuple-element.69) | copy-start | bytes 3076
  312.4 55.9 %copy-start.61 = (f32[256]{0:T(256)S(1)}, f32[256]{0:T(256)}, u32[]{:S(2)}) copy-start(f32[256]{0:T(256)} %get-tuple-element.121) | copy-start | bytes 3076
  665.8 12.2 %slice-start.2 = ((s8[6291456]{0:T(1024)(128)(4,1)}), s8[4194304]{0:T(1024)(128)(4,1)S(1)}, s32[]{:S(2)}) async-start(s8[6291456]{0:T(1024)(128)(4,1)} %bitcast.107), calls=%async_computation.18 | async-start | bytes 8388608
  668.4 16.1 %slice-start = ((s8[6291456]{0:T(1024)(128)(4,1)}), s8[4194304]{0:T(1024)(128)(4,1)S(1)}, s32[]{:S(2)}) async-start(s8[6291456]{0:T(1024)(128)(4,1)} %bitcast.105), calls=%async_computation.16 | async-start | bytes 8388608
  (61 other events, 214.9 us)
Sparse Core Ops, SparseCore 0:
  9.6 30.6 all-gather.3
  70.4 43.6 reduce-scatter.6
  116.0 27.2 all-gather.5
  161.9 43.3 reduce-scatter.10
  220.3 26.2 all-gather.7
  256.3 11.1 reduce-scatter.12
  270.3 11.6 reduce-scatter.14
  284.9 27.1 reduce-scatter.8
  315.1 25.7 reduce-scatter.16
  346.9 310.6 all-reduce.8
where the time goes:
time: 704 us; the launch traced here: 698 us
  waiting for transfers between devices  476 us (68%)
  other arithmetic  67.8 us (10%)
  matrix products  66.3 us (9%)
  blocking collectives  46.1 us (7%)
  between operations  15.3 us (2%)
  local copies, waits for them, and re-layouts  15.1 us (2%)
  starting transfers between devices  10.8 us (2%)
    psum x1, waiting for transfers between devices, per_device(): lax.psum(grad_query_w.astype(jnp.bfloat16), ('dp', 'ctx'))  287 us
    dot_general x21, matrix products, matmul(): return jnp.dot(left, right, preferred_element_type=jnp.float32)  59.2 us
    reduce_scatter x1, waiting for transfers between devices, per_device(): lax.psum_scatter(attention_terms, 'tensor', scatter_dimension=1, tiled=True)  43.7 us
    reduce_scatter x1, waiting for transfers between devices, per_device(): lax.psum_scatter(grad_normed_two, 'tensor', scatter_dimension=1, tiled=True)  41.2 us
    all_gather x1, waiting for transfers between devices, per_device(): lax.all_gather(resid_part, 'tensor', axis=1, tiled=True).astype(jnp.float32)  27 us
    reduce_scatter x1, waiting for transfers between devices, per_device(): lax.psum_scatter(grad_normed_one.astype(jnp.bfloat16), 'tensor', scatter_...  25.9 us
    all_gather x1, waiting for transfers between devices, per_device(): lax.all_gather(grad_resid.astype(jnp.bfloat16), 'tensor', axis=1, tiled=T...  25.7 us
    all_gather x1, waiting for transfers between devices, per_device(): lax.all_gather(inputs, 'tensor', axis=1, tiled=True).astype(jnp.float32)  24.9 us
  transfers between devices with their start and end apart: 10, of which 7 were waited for; matrix products, arithmetic and copies ran while one was open for 9% of the time, Pallas kernels for 0%

commit v1 on v0

--- a/solution.py
+++ b/solution.py
@@ -241,7 +241,7 @@
     grad_attention_gain = jnp.sum(grad_one_part * unit_one_part, axis=0)
     summed = (
         lax.psum(grad_attention_gain.astype(jnp.bfloat16), ("dp", "ctx")).astype(jnp.float32),
-        lax.psum(grad_query_w.astype(jnp.bfloat16), ("dp", "ctx")).astype(jnp.float32),
+        lax.psum(lax.psum(grad_query_w.astype(jnp.bfloat16), "ctx"), "dp").astype(jnp.float32),
         lax.psum(grad_key_w.astype(jnp.bfloat16), ("dp", "ctx")).astype(jnp.float32),
         lax.psum(grad_value_w.astype(jnp.bfloat16), ("dp", "ctx")).astype(jnp.float32),
         lax.psum(query_gain_total.astype(jnp.bfloat16), ("dp", "ctx")).astype(jnp.float32),

time: 704 us -> 802 us (1.14)
  waiting for transfers between devices: 476 us -> 572 us
  starting transfers between devices: 10.8 us -> 1.34 us
    psum x1 -> x3, waiting for transfers between devices: 287 us -> 362 us  [the longest x1 291 us: per_device(): lax.psum(grad_key_w.astype(jnp.bfloat16), ('dp', 'ctx')).astype(jnp.float32)]
    reduce_scatter x1, waiting for transfers between devices: 0.02 us -> 19 us  [per_device(): lax.psum_scatter(matmul(hidden, down_weight).astype(jnp.bfloat16), 'tenso...]
    reduce_scatter x1, starting transfers between devices: 10.1 us -> 0.04 us  [per_device(): lax.psum_scatter(matmul(hidden, down_weight).astype(jnp.bfloat16), 'tenso...]
  transfers between devices with their start and end apart: 10 -> 12, of which waited for: 7 -> 10; matrix products, arithmetic and copies ran while one was open for 9% -> 9% of each run, Pallas kernels for 0% -> 0%
where the time goes in v1:
time: 802 us; the launch traced here: 795 us
  waiting for transfers between devices  572 us (71%)
  other arithmetic  73 us (9%)
  matrix products  67.1 us (8%)
  blocking collectives  46.2 us (6%)
  local copies, waits for them, and re-layouts  20.9 us (3%)
  between operations  15.3 us (2%)
    psum x1, waiting for transfers between devices, per_device(): lax.psum(grad_key_w.astype(jnp.bfloat16), ('dp', 'ctx')).astype(jnp.float32)  291 us
    dot_general x21, matrix products, matmul(): return jnp.dot(left, right, preferred_element_type=jnp.float32)  59.9 us
    psum x1, waiting for transfers between devices, per_device(): lax.psum(grad_query_w.astype(jnp.bfloat16), 'ctx')  48.7 us
    reduce_scatter x1, waiting for transfers between devices, per_device(): lax.psum_scatter(attention_terms, 'tensor', scatter_dimension=1, tiled=True)  43.8 us
    reduce_scatter x1, waiting for transfers between devices, per_device(): lax.psum_scatter(grad_normed_two, 'tensor', scatter_dimension=1, tiled=True)  41.2 us
    all_gather x1, waiting for transfers between devices, per_device(): lax.all_gather(resid_part, 'tensor', axis=1, tiled=True).astype(jnp.float32)  26.9 us
    reduce_scatter x1, waiting for transfers between devices, per_device(): lax.psum_scatter(grad_normed_one.astype(jnp.bfloat16), 'tensor', scatter_...  26.8 us
    all_gather x1, waiting for transfers between devices, per_device(): lax.all_gather(grad_resid.astype(jnp.bfloat16), 'tensor', axis=1, tiled=T...  25.6 us
  transfers between devices with their start and end apart: 12, of which 10 were waited for; matrix products, arithmetic and copies ran while one was open for 9% of the time, Pallas kernels for 0%

profile of v1, /device:TPU:0, one launch (start us, length us, event | category | flops | bytes accessed | tf_op | source)
XLA Modules:
  0.0 795.4 jit_solution(17748124670958978191)
XLA Ops:
  15.3 25.0 %all-gather.4.cloned.1.call-done = bf16[256,2048]{1,0:T(8,128)(2,1)} async-done(((bf16[256,512]{1,0:T(8,128)(2,1)}), bf16[256,2048]{1,0:T(8,128)(2,1)}) %all-gather.4.cloned.1.call-update) | async-done | bytes 1048592 | tf_op jit(solution)/shard_map/all_gather | solution.py:71
  44.4 5.9 all_gather.16
  55.5 5.8 all_gather.17
  73.7 43.8 %reduce-scatter.7.cloned.1.call-done = f32[256,512]{1,0:T(8,128)} async-done(((f32[256,2048]{1,0:T(8,128)}), f32[256,512]{1,0:T(8,128)}) %reduce-scatter.7.cloned.1.call-update) | async-done | bytes 524304 | tf_op jit(solution)/shard_map/reduce_scatter | solution.py:132
  119.9 26.9 %all-gather.6.cloned.1.call-done = bf16[256,2048]{1,0:T(8,128)(2,1)} async-done(((bf16[256,512]{1,0:T(8,128)(2,1)}), bf16[256,2048]{1,0:T(8,128)(2,1)}) %all-gather.6.cloned.1.call-update) | async-done | bytes 1048592 | tf_op jit(solution)/shard_map/all_gather | solution.py:134
  149.0 5.7 fusion.33
  167.5 41.2 %reduce-scatter.11.cloned.1.call-done = f32[256,512]{1,0:T(8,128)} async-done(((f32[256,2048]{1,0:T(8,128)}), f32[256,512]{1,0:T(8,128)}) %reduce-scatter.11.cloned.1.call-update) | async-done | bytes 524304 | tf_op jit(solution)/shard_map/reduce_scatter | solution.py:158
  210.6 10.5 %psum.112 = f32[256]{0:T(256)} all-reduce(f32[256]{0:T(256)} %get-tuple-element.70), channel_id=1, replica_groups=mesh['dp'=4,'ctx'=2,'tensor'=4] {'tensor'}, use_global_device_ids=true, to_apply=%region_10.11 | all-reduce | flops 256 | bytes 2048 | tf_op jit(solution)/shard_map/psum | solution.py:160
  224.3 25.6 %all-gather.8.cloned.1.call-done = bf16[256,2048]{1,0:T(8,128)(2,1)} async-done(((bf16[256,512]{1,0:T(8,128)(2,1)}), bf16[256,2048]{1,0:T(8,128)(2,1)}) %all-gather.8.cloned.1.call-update) | async-done | bytes 1048592 | tf_op jit(solution)/shard_map/all_gather | solution.py:167
  279.5 5.7 convolution_convert_fusion.7
  292.8 5.8 convolution_convert_fusion.1
  298.6 4.6 convolution_convert_fusion.2
  303.3 48.7 %all-reduce.11.cloned.1.call-done = bf16[2048,512]{1,0:T(8,128)(2,1)} async-done(((bf16[2048,512]{1,0:T(8,128)(2,1)}), bf16[2048,512]{1,0:T(8,128)(2,1)}) %all-reduce.11.cloned.1.call-update) | async-done | bytes 2097168 | tf_op jit(solution)/shard_map/psum | solution.py:244
  352.3 4.5 convolution_convert_fusion
  363.2 19.0 %reduce-scatter.9.cloned.1.call-done = bf16[256,512]{1,0:T(8,128)(2,1)} async-done(((bf16[256,2048]{1,0:T(8,128)(2,1)}), bf16[256,512]{1,0:T(8,128)(2,1)}) %reduce-scatter.9.cloned.1.call-update) | async-done | bytes 262160 | tf_op jit(solution)/shard_map/reduce_scatter | solution.py:143
  383.9 26.8 %reduce-scatter.17.cloned.1.call-done = bf16[256,512]{1,0:T(8,128)(2,1)} async-done(((bf16[256,2048]{1,0:T(8,128)(2,1)}), bf16[256,512]{1,0:T(8,128)(2,1)}) %reduce-scatter.17.cloned.1.call-update) | async-done | bytes 262160 | tf_op jit(solution)/shard_map/reduce_scatter | solution.py:228
  411.9 9.7 %all-reduce.4 = (f32[256]{0:T(256)S(1)}, bf16[128]{0:T(256)(128)(2,1)S(1)}, bf16[128]{0:T(256)(128)(2,1)S(1)}) all-reduce(f32[256]{0:T(256)S(1)} %get-tuple-element.72, f32[128]{0:T(128)S(1)} %copy-done.63, f32[128]{0:T(128)S(1)} %copy-done.64), channel_id=1, replica_groups=mesh['dp'=4,'ctx'=2,'tensor'=4] {'tensor'}, use_global_device_ids=true, to_apply=%region_18.19 | all-reduce | flops 512 | bytes 3584 | tf_op jit(solution)/shard_map/psum | solution.py:233
  421.6 14.4 %all-reduce.5 = (bf16[512]{0:T(512)(128)(2,1)S(1)}, bf16[128]{0:T(256)(128)(2,1)S(1)}, bf16[128]{0:T(256)(128)(2,1)S(1)}, bf16[512]{0:T(512)(128)(2,1)S(1)}) all-reduce(bf16[512]{0:T(512)(128)(2,1)S(1)} %get-tuple-element.71, bf16[128]{0:T(256)(128)(2,1)S(1)} %get-tuple-element.78, ...), channel_id=1, replica_groups=mesh['dp'=4,'ctx'=2,'tensor'=4] {'dp','ctx'}, use_global_device_ids=true, to_apply=%region_20.21 | all-reduce | flops 1280 | bytes 5120 | tf_op jit(solution)/shard_map/psum | solution.py:243
  440.2 23.2 %all-reduce.13.cloned.1.call-done = bf16[2048,512]{1,0:T(8,128)(2,1)} async-done(((bf16[2048,512]{1,0:T(8,128)(2,1)}), bf16[2048,512]{1,0:T(8,128)(2,1)}) %all-reduce.13.cloned.1.call-update) | async-done | bytes 2097168 | tf_op jit(solution)/shard_map/psum | solution.py:244
  463.4 4.2 convert_element_type.251
  467.6 290.5 %all-reduce.15.cloned.1.call-done = (bf16[2048,256]{1,0:T(8,128)(2,1)}, bf16[2048,256]{1,0:T(8,128)(2,1)}, bf16[512,2048]{1,0:T(8,128)(2,1)}, bf16[2048,1536]{1,...) async-done(((bf16[2048,256]{1,0:T(8,128)(2,1)}, bf16[2048,256]{1,0:T(8,128)(2,1)}, bf16[512,2048]{1,0:T(8,128)(2,1)}, bf16[2048,1536]{1,0:T(8,128)(2,1)}, ...) | async-done | bytes 23068688 | tf_op jit(solution)/shard_map/psum | solution.py:245
  766.0 9.5 %convert_element_type.265 = f32[2048,1536]{1,0:T(8,128)} convert(bf16[2048,1536]{1,0:T(8,128)(2,1)} %get-tuple-element.100) | non-fusion elementwise | flops 3145728 | bytes 18874368 | tf_op jit(solution)/shard_map/convert_element_type | solution.py:251
  775.5 6.6 convert_element_type.267
  782.0 6.3 convert_element_type.269
  (268 shorter events, 110.2 us)
Async XLA Ops:
  7.2 64.4 %copy-start = (bf16[512,2048]{1,0:T(8,128)(2,1)S(1)}, bf16[512,2048]{1,0:T(8,128)(2,1)}, u32[]{:S(2)}) copy-start(bf16[512,2048]{1,0:T(8,128)(2,1)} %param.25) | copy-start | bytes 6291460
  7.2 33.1 %all-gather.4.cloned.1.call-start = ((), (), s32[]{:S(2)}) async-start(), calls=%async_computation.6 | async-start | bytes 1310720 | tf_op jit(solution)/shard_map/all_gather | solution.py:71
  7.9 109.6 %reduce-scatter.7.cloned.1.call-start = ((), (), s32[]{:S(2)}) async-start(), calls=%async_computation.7 | async-start | bytes 2621440 | tf_op jit(solution)/shard_map/reduce_scatter | solution.py:132
  8.6 57.2 %copy-start.59 = (f32[128]{0:T(128)}, f32[128]{0:T(128)S(1)}, u32[]{:S(2)}) copy-start(f32[128]{0:T(128)S(1)} %convert_element_type.215) | copy-start | bytes 1540
  11.2 50.0 %copy-start.56 = (f32[2048]{0:T(1024)}, f32[2048]{0:T(1024)S(1)}, u32[]{:S(2)}) copy-start(f32[2048]{0:T(1024)S(1)} %convert_element_type.208) | copy-start | bytes 24580
  11.7 32.6 %copy-start.17 = (f32[256,64]{1,0:T(8,128)}, f32[256,64]{1,0:T(8,128)S(1)}, u32[]{:S(2)}) copy-start(f32[256,64]{1,0:T(8,128)S(1)} %get-tuple-element.119) | copy-start | bytes 196612
  73.7 43.8 %copy-start.30 = (bf16[256,512]{1,0:T(8,128)(2,1)S(1)}, bf16[256,512]{1,0:T(8,128)(2,1)}, u32[]{:S(2)}) copy-start(bf16[256,512]{1,0:T(8,128)(2,1)} %param.15) | copy-start | bytes 786436
  73.7 46.2 %copy-start.52 = (bf16[2048]{0:T(1024)(128)(2,1)S(1)}, bf16[2048]{0:T(1024)(128)(2,1)}, u32[]{:S(2)}) copy-start(bf16[2048]{0:T(1024)(128)(2,1)} %param.26) | copy-start | bytes 12292
  73.7 73.1 %all-gather.6.cloned.1.call-start = ((), (), s32[]{:S(2)}) async-start(), calls=%async_computation.8 | async-start | bytes 1310720 | tf_op jit(solution)/shard_map/all_gather | solution.py:134
  119.3 89.4 %reduce-scatter.11.cloned.1.call-start = ((), (), s32[]{:S(2)}) async-start(), calls=%async_computation.10 | async-start | bytes 2621440 | tf_op jit(solution)/shard_map/reduce_scatter | solution.py:158
  165.2 84.8 %all-gather.8.cloned.1.call-start = ((), (), s32[]{:S(2)}) async-start(), calls=%async_computation.11 | async-start | bytes 1310720 | tf_op jit(solution)/shard_map/all_gather | solution.py:167
  223.6 61.7 %reduce-scatter.13.cloned.1.call-start = ((), (), s32[]{:S(2)}) async-start(), calls=%async_computation.12 | async-start | bytes 393216 | tf_op jit(solution)/shard_map/reduce_scatter | solution.py:208
  260.2 28.7 %reduce-scatter.15.cloned.1.call-start = ((), (), s32[]{:S(2)}) async-start(), calls=%async_computation.13 | async-start | bytes 393216 | tf_op jit(solution)/shard_map/reduce_scatter | solution.py:211
  274.9 77.1 %all-reduce.11.cloned.1.call-start = ((), (), s32[]{:S(2)}) async-start(), calls=%async_computation.15 | async-start | bytes 4194304 | tf_op jit(solution)/shard_map/psum | solution.py:244
  279.4 102.7 %reduce-scatter.9.cloned.1.call-start = ((), (), s32[]{:S(2)}) async-start(), calls=%async_computation.9 | async-start | bytes 1310720 | tf_op jit(solution)/shard_map/reduce_scatter | solution.py:143
  285.2 125.5 %reduce-scatter.17.cloned.1.call-start = ((), (), s32[]{:S(2)}) async-start(), calls=%async_computation.14 | async-start | bytes 1310720 | tf_op jit(solution)/shard_map/reduce_scatter | solution.py:228
  292.7 170.7 %all-reduce.13.cloned.1.call-start = ((), (), s32[]{:S(2)}) async-start(), calls=%async_computation.16 | async-start | bytes 4194304 | tf_op jit(solution)/shard_map/psum | solution.py:244
  303.2 49.0 %copy-start.24 = (bf16[256,2048]{1,0:T(8,128)(2,1)S(1)}, bf16[256,2048]{1,0:T(8,128)(2,1)}, u32[]{:S(2)}) copy-start(bf16[256,2048]{1,0:T(8,128)(2,1)} %param.16) | copy-start | bytes 3145732
  303.3 49.0 %copy-start.26 = (bf16[256,1536]{1,0:T(8,128)(2,1)S(1)}, bf16[256,1536]{1,0:T(8,128)(2,1)}, u32[]{:S(2)}) copy-start(bf16[256,1536]{1,0:T(8,128)(2,1)} %get-tuple-element.107) | copy-start | bytes 2359300
  352.0 406.1 %all-reduce.15.cloned.1.call-start = ((), (), s32[]{:S(2)}) async-start(), calls=%async_computation.17 | async-start | bytes 46137344 | tf_op jit(solution)/shard_map/psum | solution.py:245
  362.9 48.9 %copy-start.63 = (f32[128]{0:T(128)S(1)}, f32[128]{0:T(128)}, u32[]{:S(2)}) copy-start(f32[128]{0:T(128)} %get-tuple-element.73) | copy-start | bytes 1540
  362.9 48.9 %copy-start.64 = (f32[128]{0:T(128)S(1)}, f32[128]{0:T(128)}, u32[]{:S(2)}) copy-start(f32[128]{0:T(128)} %get-tuple-element.75) | copy-start | bytes 1540
  362.9 58.6 %copy-start.62 = (bf16[512]{0:T(512)(128)(2,1)S(1)}, bf16[512]{0:T(512)(128)(2,1)}, u32[]{:S(2)}) copy-start(bf16[512]{0:T(512)(128)(2,1)} %get-tuple-element.69) | copy-start | bytes 3076
  363.0 75.2 %copy-start.61 = (f32[256]{0:T(256)S(1)}, f32[256]{0:T(256)}, u32[]{:S(2)}) copy-start(f32[256]{0:T(256)} %get-tuple-element.120) | copy-start | bytes 3076
  (63 other events, 281.2 us)
Sparse Core Ops, SparseCore 0:
  9.6 30.6 all-gather.3
  73.8 43.6 reduce-scatter.6
  119.5 27.2 all-gather.5
  165.3 43.3 reduce-scatter.10
  223.7 26.2 all-gather.7
  260.3 11.1 reduce-scatter.12
  275.0 11.1 reduce-scatter.14
  289.0 62.9 all-reduce.10
  355.0 27.1 reduce-scatter.8
  384.9 25.7 reduce-scatter.16
  413.2 50.2 all-reduce.12
  469.3 288.7 all-reduce.14
